TPU v7x, 128 devices: a whole 4x4x4 slice. The times are simulated.
128 devices in a mesh: row: 8 (over y, core), col: 16 (over z, x).
Axes of the slice: x: 4, y: 4, z: 4, core: 2. Of those that a mesh axis runs over, the one named last changes fastest.
Arguments:
- kernel_panel: float32 [64, 32768], P(None, ('row', 'col')), may hold values from -4 to 16, as said below
- kernel_slab: float32 [32768, 4096], P('row', 'col'), may hold values from -4 to 20, as said below
- targets: float32 [256, 32768], P(None, ('row', 'col')), may hold values from -6 to 6
Outputs:
- updated_slab: float32 [32768, 4096], P('row', 'col')
- solved_targets: float32 [256, 32768], P('col', 'row')
- panel_factor: float32 [64, 32768], P(None, ('row', 'col'))
Inputs may be any that keep to these rules, and one draw needn't show every extreme that they name: kernel_panel[:, 0:64] is symmetric and positive definite. `kernel_slab`: rows 0 to 63 equal kernel_panel[:, 32768 - 4096 : 32768]; the last 4096 rows form a symmetric matrix.
All inputs are finite; a program needn't handle non-finite values.
Results may differ from a plain program's by a relative error of at most 0.00018.
Values sent between devices are 32-bit elements; how exact they have to be, the bound alone decides.
No kernel may reach another device: no remote copies, remote signals or barrier semaphores. Data moves between devices by JAX's collectives and lax.ppermute only.
A program may use at most 64 MiB of HBM per device.

v0:
```python
import jax
import jax.numpy as jnp
from jax import lax
from jax.sharding import PartitionSpec as P


def spread(block, axis, source):
    block = jnp.where(lax.axis_index(axis) == source, block, jnp.zeros_like(block))
    return lax.psum(block, axis)


def lower_solve(factor, values):
    return jax.scipy.linalg.solve_triangular(factor, values, lower=True)


def body(kernel_panel, kernel_slab, targets):
    highest = lax.Precision.HIGHEST
    panel_width = kernel_panel.shape[0]
    row_count = lax.axis_size("row")
    row_index = lax.axis_index("row")
    flat_index = lax.axis_index(("row", "col"))
    corner_rows = jnp.concatenate([kernel_panel[:, :panel_width], targets[:, :panel_width]], 0)
    shared = spread(corner_rows, ("row", "col"), 0)
    lower_factor = jnp.linalg.cholesky(shared[:panel_width])
    panel_factor = lower_solve(lower_factor, kernel_panel)
    gathered = lax.all_gather(panel_factor, "col", axis=1, tiled=True)
    slab_factor = spread(panel_factor, "row", row_count - 1)
    product = lax.dot_general(
        gathered,
        slab_factor,
        (((0,), (0,)), ((), ())),
        precision=highest,
        preferred_element_type=jnp.float32,
    )
    update = kernel_slab - product
    head_rows = jnp.where(row_index == 0, slab_factor, update[:panel_width])
    updated_slab = jnp.concatenate([head_rows, update[panel_width:]], 0)
    solved_lead = lower_solve(lower_factor, shared[panel_width:].T).T
    result = targets - jnp.dot(
        solved_lead, panel_factor, precision=highest, preferred_element_type=jnp.float32
    )
    head_cols = jnp.where(flat_index == 0, solved_lead, result[:, :panel_width])
    result = jnp.concatenate([head_cols, result[:, panel_width:]], 1)
    solved_targets = lax.all_to_all(result, "col", split_axis=0, concat_axis=1, tiled=True)
    return (updated_slab, solved_targets, panel_factor)


def solution(mesh):
    in_specs = (P(None, ("row", "col")), P("row", "col"), P(None, ("row", "col")))
    out_specs = (P("row", "col"), P("col", "row"), P(None, ("row", "col")))
    return jax.shard_map(body, mesh=mesh, in_specs=in_specs, out_specs=out_specs, check_vma=False)
```

profile of v0, /device:TPU:0, one launch (start us, length us, event | category | flops | bytes accessed | tf_op | source)
XLA Modules:
  0.0 286.8 jit_solution(15664791899250229156)
XLA Ops:
  7.2 0.8 slice.34
  8.1 1.1 copy.17
  9.2 0.7 maximum_select_fusion
  10.0 143.3 %all-reduce.3.cloned.1.call-done = f32[320,64]{0,1:T(8,128)} async-done(((f32[320,64]{0,1:T(8,128)}), f32[320,64]{0,1:T(8,128)}) %all-reduce.3.cloned.1.call-update) | async-done | bytes 81936 | tf_op jit(solution)/shard_map/psum | solution.py:9
  153.3 0.8 slice.43
  154.1 0.8 fusion.5
  154.9 5.8 %cholesky.18 = f32[64,64]{1,0:T(8,128)S(1)} custom-call(f32[64,64]{1,0:T(8,128)S(1)} %fusion.5), custom_call_target="Cholesky" | custom-call | tf_op jit(solution)/shard_map/jit(cholesky)/cholesky | solution.py:24
  160.8 0.6 compare_reduce_fusion
  161.4 0.7 fusion.1
  162.1 4.9 %custom-call.7 = f32[1,64,64]{1,2,0:T(8,128)S(1)} custom-call(f32[1,64,64]{2,1,0:T(8,128)S(1)} %fusion.1), custom_call_target="InvertDiagBlocksLowerTriangular" | custom-call | tf_op jit(solution)/shard_map/jit(_solve_triangular)/triangular_solve | solution.py:13
  167.0 1.8 broadcast_select_fusion
  168.8 0.7 all-gather.2.cloned.1.call-update
  169.5 1.2 fusion
  170.7 1.3 convolution_subtract_fusion.1
  172.0 0.8 copy.20
  172.9 5.6 %all-to-all-start = ((f32[16,16,256]{2,1,0:T(8,128)}), f32[16,16,256]{2,1,0:T(8,128)S(1)}, u32[]{:S(2)}, u32[]{:S(2)}) async-start(f32[16,16,256]{2,1,0:T(8,128)} %bitcast.7), calls=%async_computation | async-start | bytes 524288 | tf_op jit(solution)/shard_map/all_to_all | solution.py:44
  178.5 8.7 %all-to-all-done = f32[16,16,256]{2,1,0:T(8,128)S(1)} async-done(((f32[16,16,256]{2,1,0:T(8,128)}), f32[16,16,256]{2,1,0:T(8,128)S(1)}, u32[]{:S(2)}, u32[]{:S(2)}) %all-to-all-start) | async-done | bytes 262176 | tf_op jit(solution)/shard_map/all_to_all | solution.py:44
  187.2 0.7 copy.23
  187.9 38.0 %all-reduce.5.cloned.1.call-done = f32[64,256]{1,0:T(8,128)} async-done(((f32[64,256]{1,0:T(8,128)}), f32[64,256]{1,0:T(8,128)}) %all-reduce.5.cloned.1.call-update) | async-done | bytes 65552 | tf_op jit(solution)/shard_map/psum | solution.py:9
  225.9 45.2 %all-gather.2.cloned.1.call-done = f32[64,4096]{1,0:T(8,128)} async-done(((f32[64,256]{1,0:T(8,128)}), f32[64,4096]{1,0:T(8,128)}) %all-gather.2.cloned.1.call-update) | async-done | bytes 1048592 | tf_op jit(solution)/shard_map/all_gather | solution.py:26
  271.1 6.0 %convolution_subtract_fusion = f32[4096,256]{1,0:T(8,128)S(1)} fusion(f32[4096,256]{1,0:T(8,128)} %param.6, f32[64,4096]{1,0:T(8,128)} %all-gather.2.cloned.1.call-done, f32[64,256]{1,0:T(8,128)} %all-reduce.5.cloned.1.call-done), kind=kOutput, calls=%fused_computation | convolution fusion | flops 806354944 | bytes 9502720 | tf_op jit(solution)/shard_map/dot_general | solution.py:28
  277.1 0.3 slice.45
  277.4 0.6 copy-done
  278.0 2.3 pad_maximum_fusion
  (14 shorter events, 0.4 us)
Async XLA Ops:
  7.2 146.1 %all-reduce.3.cloned.1.call-start = ((), (), s32[]{:S(2)}) async-start(), calls=%async_computation.1 | async-start | bytes 196608 | tf_op jit(solution)/shard_map/psum | solution.py:9
  9.9 216.0 %all-reduce.5.cloned.1.call-start = ((), (), s32[]{:S(2)}) async-start(), calls=%async_computation.2 | async-start | bytes 131072 | tf_op jit(solution)/shard_map/psum | solution.py:9
  168.8 102.3 %all-gather.2.cloned.1.call-start = ((), (), s32[]{:S(2)}) async-start(), calls=%async_computation.3 | async-start | bytes 1114112 | tf_op jit(solution)/shard_map/all_gather | solution.py:26
  172.9 14.3 %all-to-all-start = ((f32[16,16,256]{2,1,0:T(8,128)}), f32[16,16,256]{2,1,0:T(8,128)S(1)}, u32[]{:S(2)}, u32[]{:S(2)}) async-start(f32[16,16,256]{2,1,0:T(8,128)} %bitcast.7), calls=%async_computation | async-start | bytes 524288 | tf_op jit(solution)/shard_map/all_to_all | solution.py:44
  277.1 0.8 copy-start
Sparse Core Ops, SparseCore 0:
  13.3 139.9 all-reduce.2
  168.9 56.9 all-reduce.4
  228.6 42.4 all-gather.1
where the time goes:
time: 287 us
  waiting for transfers between devices  236 us (82%)
  other arithmetic  15.9 us (6%)
  between operations  13.9 us (5%)
  matrix products  10.2 us (4%)
  starting transfers between devices  5.75 us (2%)
  local copies, waits for them, and re-layouts  5.16 us (2%)
    psum x2, waiting for transfers between devices, spread(): return lax.psum(block, axis)  181 us
    all_gather x1, waiting for transfers between devices, body(): gathered = lax.all_gather(panel_factor, 'col', axis=1, tiled=True)  45.2 us
    all_to_all x1, waiting for transfers between devices, body(): lax.all_to_all(result, 'col', split_axis=0, concat_axis=1, tiled=True)  8.69 us
    another operation x3, other arithmetic, body(): lower_factor = jnp.linalg.cholesky(shared[:panel_width])  6.52 us
    dot_general x1, matrix products, body(): lax.dot_general(gathered, slab_factor, (((0,), (0,)), ((), ())), precisio...  6 us
  transfers between devices with their start and end apart: 4, of which 4 were waited for; matrix products, arithmetic and copies ran while one was open for 1% of the time, Pallas kernels for 0%

commit v1 on v0

--- a/solution.py
+++ b/solution.py
@@ -23,7 +23,9 @@
     shared = spread(corner_rows, ("row", "col"), 0)
     lower_factor = jnp.linalg.cholesky(shared[:panel_width])
     panel_factor = lower_solve(lower_factor, kernel_panel)
-    gathered = lax.all_gather(panel_factor, "col", axis=1, tiled=True)
+    gathered = jnp.concatenate(
+        lax.all_to_all(jnp.stack([panel_factor] * lax.axis_size("col")), "col", 0, 0), axis=1
+    )
     slab_factor = spread(panel_factor, "row", row_count - 1)
     product = lax.dot_general(
         gathered,

time: 287 us -> 267 us (0.930)
  waiting for transfers between devices: 236 us -> 204 us
  blocking collectives: 0 us -> 14.1 us
    all_gather x1 -> x0, waiting for transfers between devices: 45.2 us -> none  [body(): gathered = lax.all_gather(panel_factor, 'col', axis=1, tiled=True)]
    all_to_all x0 -> x1, blocking collectives: none -> 14.1 us  [body(): lax.all_to_all(result, 'col', split_axis=0, concat_axis=1, tiled=True)]
    psum x2, waiting for transfers between devices: 181 us -> 189 us  [spread(): return lax.psum(block, axis)]
    all_to_all x1, waiting for transfers between devices: 8.69 us -> 14.4 us  [body(): lax.all_to_all(jnp.stack([panel_factor] * lax.axis_size('col')), 'col', 0...]
  transfers between devices with their start and end apart: 4 -> 3, of which waited for: 4 -> 3; matrix products, arithmetic and copies ran while one was open for 1% -> 0% of each run, Pallas kernels for 0% -> 0%
where the time goes in v1:
time: 267 us
  waiting for transfers between devices  204 us (76%)
  other arithmetic  15.9 us (6%)
  between operations  14.2 us (5%)
  blocking collectives  14.1 us (5%)
  matrix products  8.66 us (3%)
  local copies, waits for them, and re-layouts  5.62 us (2%)
  starting transfers between devices  3.74 us (1%)
    psum x2, waiting for transfers between devices, spread(): return lax.psum(block, axis)  189 us
    all_to_all x1, waiting for transfers between devices, body(): lax.all_to_all(jnp.stack([panel_factor] * lax.axis_size('col')), 'col', 0...  14.4 us
    all_to_all x1, blocking collectives, body(): lax.all_to_all(result, 'col', split_axis=0, concat_axis=1, tiled=True)  14.1 us
    another operation x3, other arithmetic, body(): lower_factor = jnp.linalg.cholesky(shared[:panel_width])  6.52 us
    another operation x2, other arithmetic, lower_solve(): return jax.scipy.linalg.solve_triangular(factor, values, lower=True)  5.55 us
  transfers between devices with their start and end apart: 3, of which 3 were waited for; matrix products, arithmetic and copies ran while one was open for 0% of the time, Pallas kernels for 0%

profile of v1, /device:TPU:0, one launch (start us, length us, event | category | flops | bytes accessed | tf_op | source)
XLA Modules:
  0.0 266.7 jit_solution(633331564421748093)
XLA Ops:
  7.2 0.8 slice.34
  8.1 1.1 copy.23
  9.2 0.7 maximum_select_fusion
  9.9 143.4 %all-reduce.3.cloned.1.call-done = f32[320,64]{0,1:T(8,128)} async-done(((f32[320,64]{0,1:T(8,128)}), f32[320,64]{0,1:T(8,128)}) %all-reduce.3.cloned.1.call-update) | async-done | bytes 81936 | tf_op jit(solution)/shard_map/psum | solution.py:9
  153.3 0.8 slice.43
  154.1 0.8 fusion.5
  154.9 5.8 %cholesky.18 = f32[64,64]{1,0:T(8,128)S(1)} custom-call(f32[64,64]{1,0:T(8,128)S(1)} %fusion.5), custom_call_target="Cholesky" | custom-call | tf_op jit(solution)/shard_map/jit(cholesky)/cholesky | solution.py:24
  160.8 0.6 compare_reduce_fusion
  161.4 0.7 fusion.1
  162.1 4.9 %custom-call.7 = f32[1,64,64]{1,2,0:T(8,128)S(1)} custom-call(f32[1,64,64]{2,1,0:T(8,128)S(1)} %fusion.1), custom_call_target="InvertDiagBlocksLowerTriangular" | custom-call | tf_op jit(solution)/shard_map/jit(_solve_triangular)/triangular_solve | solution.py:13
  167.0 1.7 broadcast_select_fusion
  168.7 1.2 fusion
  169.9 0.4 convolution_subtract_fusion.1
  170.6 14.1 %all_to_all.24 = f32[16,16,256]{2,1,0:T(8,128)S(1)} all-to-all(f32[16,16,256]{2,1,0:T(8,128)S(1)} %bitcast.35), channel_id=1, replica_groups=mesh['row'=8,'col'=16] {'col'}, dimensions={0} | all-to-all | bytes 524288 | tf_op jit(solution)/shard_map/all_to_all | solution.py:46
  184.7 1.1 stack.2
  185.8 3.7 %all-to-all-start = ((f32[16,64,256]{2,1,0:T(8,128)}), f32[16,64,256]{2,1,0:T(8,128)S(1)}, u32[]{:S(2)}, u32[]{:S(2)}) async-start(f32[16,64,256]{2,1,0:T(8,128)} %stack.2), calls=%async_computation | async-start | bytes 2097152 | tf_op jit(solution)/shard_map/all_to_all | solution.py:27
  189.5 0.7 all-reduce.5.cloned.1.call-update
  190.2 0.7 copy.31
  190.9 14.4 %all-to-all-done = f32[16,64,256]{2,1,0:T(8,128)S(1)} async-done(((f32[16,64,256]{2,1,0:T(8,128)}), f32[16,64,256]{2,1,0:T(8,128)S(1)}, u32[]{:S(2)}, u32[]{:S(2)}) %all-to-all-start) | async-done | bytes 1048608 | tf_op jit(solution)/shard_map/all_to_all | solution.py:27
  205.4 45.9 %all-reduce.5.cloned.1.call-done = f32[64,256]{1,0:T(8,128)} async-done(((f32[64,256]{1,0:T(8,128)}), f32[64,256]{1,0:T(8,128)}) %all-reduce.5.cloned.1.call-update) | async-done | bytes 65552 | tf_op jit(solution)/shard_map/psum | solution.py:9
  251.4 5.3 %convolution_subtract_fusion = f32[4096,256]{1,0:T(8,128)S(1)} fusion(f32[4096,256]{1,0:T(8,128)} %param.6, f32[64,4096]{1,0:T(8,128)S(1)} %bitcast.32, f32[64,256]{1,0:T(8,128)} %all-reduce.5.cloned.1.call-done), kind=kOutput, calls=%fused_computation | convolution fusion | flops 806354944 | bytes 9502720 | tf_op jit(solution)/shard_map/dot_general | solution.py:30
  256.7 0.3 slice.45
  257.0 0.6 copy-done.1
  257.5 2.3 pad_maximum_fusion
  (16 shorter events, 0.6 us)
Async XLA Ops:
  7.2 146.1 %all-reduce.3.cloned.1.call-start = ((), (), s32[]{:S(2)}) async-start(), calls=%async_computation.2 | async-start | bytes 196608 | tf_op jit(solution)/shard_map/psum | solution.py:9
  168.7 36.7 %copy-start = (f32[64,256]{1,0:T(8,128)}, f32[64,256]{1,0:T(8,128)S(1)}, u32[]{:S(2)}) copy-start(f32[64,256]{1,0:T(8,128)S(1)} %get-tuple-element.5) | copy-start | bytes 196612
  185.8 19.5 %all-to-all-start = ((f32[16,64,256]{2,1,0:T(8,128)}), f32[16,64,256]{2,1,0:T(8,128)S(1)}, u32[]{:S(2)}, u32[]{:S(2)}) async-start(f32[16,64,256]{2,1,0:T(8,128)} %stack.2), calls=%async_computation | async-start | bytes 2097152 | tf_op jit(solution)/shard_map/all_to_all | solution.py:27
  189.4 61.9 %all-reduce.5.cloned.1.call-start = ((), (), s32[]{:S(2)}) async-start(), calls=%async_computation.3 | async-start | bytes 131072 | tf_op jit(solution)/shard_map/psum | solution.py:9
  256.7 0.8 copy-start.1
Sparse Core Ops, SparseCore 0:
  13.3 139.9 all-reduce.2
  192.7 58.6 all-reduce.4
